TPU v7x, 32 devices: a whole 2x2x4 slice. The times are simulated.
32 devices in a mesh: section: 4 (over z), row: 2 (over y), col: 4 (over x, core).
Axes of the slice: x: 2, y: 2, z: 4, core: 2. Of those that a mesh axis runs over, the one named last changes fastest.
Arguments:
- tokens: bfloat16 [4, 128, 3072], P('section', 'col', 'row'), may hold values from -6 to 6
- weights: bfloat16 [4, 3072, 12288], P('section', 'row', 'col'), may hold values from -0.109375 to 0.109375
- hidden_grads: bfloat16 [4, 128, 12288], P('section', 'row', 'col'), may hold values from -1.5 to 1.5
Outputs:
- hidden: bfloat16 [4, 128, 12288], P('section', 'row', 'col')
- weight_grad: bfloat16 [4, 3072, 12288], P('section', 'row', 'col')
- passed_grad: bfloat16 [4, 128, 3072], P('section', 'col', 'row')
All inputs are finite; a program needn't handle non-finite values.
Results may differ from a plain program's by a relative error of at most 0.0052.
Values may be sent and summed in bfloat16 or wider, within the bound.
No kernel may reach another device: no remote copies, remote signals or barrier semaphores. Data moves between devices by JAX's collectives and lax.ppermute only.
A program may use at most 64 MiB of HBM per device.

v0:
```python
import jax
import jax.numpy as jnp
from jax import lax
from jax.sharding import PartitionSpec as P


def shifted(value, axis, steps):
    count = lax.axis_size(axis)
    leading, last = (max(0, -steps), min(count, count - steps))
    return lax.ppermute(value, axis, [(source, source + steps) for source in range(leading, last)])


def on_device(tokens, weights, hidden_grads):
    token_tile = tokens[0]
    weight_tile = weights[0]
    grad_tile = hidden_grads[0]
    tokens_all = lax.all_gather(token_tile, "col", axis=0, tiled=True)
    hidden_sum = lax.psum_scatter(
        jnp.dot(tokens_all, weight_tile, preferred_element_type=jnp.float32).astype(jnp.bfloat16),
        "row",
        scatter_dimension=0,
        tiled=True,
    )
    grad_piece = lax.all_gather(grad_tile, "row", axis=0, tiled=True)
    weight_total = lax.dot_general(
        tokens_all, grad_piece, (((0,), (0,)), ((), ())), preferred_element_type=jnp.float32
    )
    input_piece = lax.dot_general(
        grad_piece, weight_tile, (((1,), (1,)), ((), ())), preferred_element_type=jnp.float32
    )
    weight_grad = weight_total.astype(jnp.bfloat16)
    input_grad = lax.psum_scatter(input_piece, "col", scatter_dimension=0, tiled=True).astype(
        jnp.bfloat16
    )
    passed_grad = shifted(input_grad, "section", -1)
    return (hidden_sum[None], weight_grad[None], passed_grad[None])


def solution(mesh):
    in_specs = (P("section", "col", "row"), P("section", "row", "col"), P("section", "row", "col"))
    out_specs = (P("section", "row", "col"), P("section", "row", "col"), P("section", "col", "row"))
    return jax.shard_map(
        on_device, mesh=mesh, in_specs=in_specs, out_specs=out_specs, check_vma=False
    )
```

profile of v0, /device:TPU:0, one launch (start us, length us, event | category | flops | bytes accessed | tf_op | source)
XLA Modules:
  0.0 80.7 jit_solution(3190279994158967588)
XLA Ops:
  7.2 0.0 copy-start
  7.2 0.0 reduce-scatter.5.cloned.1.call-start
  7.2 13.0 %all-gather.1 = bf16[1,128,3072]{2,1,0:T(8,128)(2,1)S(1)} all-gather(bf16[1,64,3072]{2,1,0:T(8,128)(2,1)} %param.5), channel_id=3, replica_groups=mesh['section'=4,'row'=2,'col'=4] {'row'}, dimensions={1}, use_global_device_ids=true | all-gather | bytes 1179648 | tf_op jit(solution)/shard_map/all_gather | solution.py:24
  20.2 7.8 %fusion.1 = f32[128,1536]{1,0:T(8,128)} fusion(bf16[1,1536,3072]{2,1,0:T(8,128)(2,1)} %param.4, bf16[1,128,3072]{2,1,0:T(8,128)(2,1)S(1)} %all-gather.1), kind=kOutput, calls=%fused_computation.2 | convolution fusion | flops 1207959552 | bytes 11010048 | tf_op jit(solution)/shard_map/dot_general | solution.py:28
  28.0 0.0 reduce-scatter.5.cloned.1.call-update
  28.0 0.0 reduce-scatter.3.cloned.1.call-start
  28.1 0.0 copy-done
  28.1 6.6 %all-gather = bf16[1,128,1536]{2,1,0:T(8,128)(2,1)S(1)} all-gather(bf16[1,32,1536]{2,1,0:T(8,128)(2,1)S(1)} %copy-done), channel_id=2, replica_groups=mesh['section'=4,'row'=2,'col'=4] {'col'}, dimensions={1}, use_global_device_ids=true | all-gather | bytes 491520 | tf_op jit(solution)/shard_map/all_gather | solution.py:17
  34.7 6.2 %fusion.5 = bf16[128,3072]{1,0:T(8,128)(2,1)} fusion(bf16[1,1536,3072]{2,1,0:T(8,128)(2,1)} %param.4, bf16[1,128,1536]{2,1,0:T(8,128)(2,1)S(1)} %all-gather), kind=kOutput, calls=%fused_computation.6 | convolution fusion | flops 1208352768 | bytes 10616832 | tf_op jit(solution)/shard_map/dot_general | solution.py:19
  41.0 0.0 reduce-scatter.3.cloned.1.call-update
  41.0 11.9 %reduce-scatter.5.cloned.1.call-done = f32[32,1536]{1,0:T(8,128)} async-done(((f32[128,1536]{1,0:T(8,128)}), f32[32,1536]{1,0:T(8,128)}) %reduce-scatter.5.cloned.1.call-update) | async-done | bytes 196624 | tf_op jit(solution)/shard_map/reduce_scatter | solution.py:32
  52.9 0.9 %convert_element_type.11 = bf16[32,1536]{1,0:T(8,128)(2,1)S(1)} convert(f32[32,1536]{1,0:T(8,128)} %reduce-scatter.5.cloned.1.call-done) | non-fusion elementwise | flops 49152 | bytes 294912 | tf_op jit(solution)/shard_map/convert_element_type | solution.py:32
  53.8 1.3 %collective-permute-start = (bf16[32,1536]{1,0:T(8,128)(2,1)S(1)}, bf16[32,1536]{1,0:T(8,128)(2,1)S(1)}, u32[]{:S(2)}, u32[]{:S(2)}) collective-permute-start(bf16[32,1536]{1,0:T(8,128)(2,1)S(1)} %convert_element_type.11), channel_id=1, source_target_pairs={{8,0},{16,8},{24,16},{9,1},{17,9},{25,17},{10,2},{18,10},{26,18},{... | collective-permute-start | bytes 294920 | tf_op jit(solution)/shard_map/ppermute | solution.py:10
  55.1 5.2 %fusion = bf16[1,1536,3072]{2,1,0:T(8,128)(2,1)} fusion(bf16[1,128,3072]{2,1,0:T(8,128)(2,1)S(1)} %all-gather.1, bf16[1,128,1536]{2,1,0:T(8,128)(2,1)S(1)} %all-gather), kind=kOutput, calls=%fused_computation.1 | convolution fusion | flops 1212678144 | bytes 10616832 | tf_op jit(solution)/shard_map/dot_general | solution.py:25
  60.3 0.0 collective-permute-done
  60.3 12.9 %reduce-scatter.3.cloned.1.call-done = bf16[64,3072]{1,0:T(8,128)(2,1)} async-done(((bf16[128,3072]{1,0:T(8,128)(2,1)}), bf16[64,3072]{1,0:T(8,128)(2,1)}) %reduce-scatter.3.cloned.1.call-update) | async-done | bytes 393232 | tf_op jit(solution)/shard_map/reduce_scatter | solution.py:18
  73.3 0.6 copy.7
Async XLA Ops:
  7.2 20.9 %copy-start = (bf16[1,32,1536]{2,1,0:T(8,128)(2,1)S(1)}, bf16[1,32,1536]{2,1,0:T(8,128)(2,1)}, u32[]{:S(2)}) copy-start(bf16[1,32,1536]{2,1,0:T(8,128)(2,1)} %param.3) | copy-start | bytes 294916
  7.2 45.7 %reduce-scatter.5.cloned.1.call-start = ((), (), s32[]{:S(2)}) async-start(), calls=%async_computation.3 | async-start | bytes 983040 | tf_op jit(solution)/shard_map/reduce_scatter | solution.py:32
  28.0 45.2 %reduce-scatter.3.cloned.1.call-start = ((), (), s32[]{:S(2)}) async-start(), calls=%async_computation.2 | async-start | bytes 1179648 | tf_op jit(solution)/shard_map/reduce_scatter | solution.py:18
  53.8 6.5 %collective-permute-start = (bf16[32,1536]{1,0:T(8,128)(2,1)S(1)}, bf16[32,1536]{1,0:T(8,128)(2,1)S(1)}, u32[]{:S(2)}, u32[]{:S(2)}) collective-permute-start(bf16[32,1536]{1,0:T(8,128)(2,1)S(1)} %convert_element_type.11), channel_id=1, source_target_pairs={{8,0},{16,8},{24,16},{9,1},{17,9},{25,17},{10,2},{18,10},{26,18},{... | collective-permute-start | bytes 294920 | tf_op jit(solution)/shard_map/ppermute | solution.py:10
Sparse Core Ops, SparseCore 0:
  28.2 24.6 reduce-scatter.4
  55.8 17.4 reduce-scatter.2
where the time goes:
time: 81 us; the launch traced here: 80.7 us
  waiting for transfers between devices  24.9 us (31%)
  blocking collectives  19.7 us (24%)
  matrix products  19.2 us (24%)
  between operations  14.1 us (17%)
  starting transfers between devices  1.37 us (2%)
  other arithmetic  0.94 us (1%)
    all_gather x1, blocking collectives, on_device(): grad_piece = lax.all_gather(grad_tile, 'row', axis=0, tiled=True)  13 us
    reduce_scatter x1, waiting for transfers between devices, on_device(): lax.psum_scatter(jnp.dot(tokens_all, weight_tile, preferred_element_type=...  12.9 us
    reduce_scatter x1, waiting for transfers between devices, on_device(): lax.psum_scatter(input_piece, 'col', scatter_dimension=0, tiled=True)  11.9 us
    dot_general x1, matrix products, on_device(): lax.dot_general(grad_piece, weight_tile, (((1,), (1,)), ((), ())), prefer...  7.78 us
    all_gather x1, blocking collectives, on_device(): tokens_all = lax.all_gather(token_tile, 'col', axis=0, tiled=True)  6.64 us
    dot_general x1, matrix products, on_device(): jnp.dot(tokens_all, weight_tile, preferred_element_type=jnp.float32)  6.23 us
    dot_general x1, matrix products, on_device(): lax.dot_general(tokens_all, grad_piece, (((0,), (0,)), ((), ())), preferr...  5.17 us
  transfers between devices with their start and end apart: 3, of which 2 were waited for; matrix products, arithmetic and copies ran while one was open for 15% of the time, Pallas kernels for 0%

commit v1 on v0

--- a/solution.py
+++ b/solution.py
@@ -2,6 +2,12 @@
 import jax.numpy as jnp
 from jax import lax
 from jax.sharding import PartitionSpec as P
+
+
+def in_order(pieces, dim):
+    shape = list(pieces.shape[1:])
+    shape[dim] *= pieces.shape[0]
+    return jnp.moveaxis(pieces, 0, dim).reshape(shape)
 
 
 def shifted(value, axis, steps):
@@ -14,7 +20,19 @@
     token_tile = tokens[0]
     weight_tile = weights[0]
     grad_tile = hidden_grads[0]
-    tokens_all = lax.all_gather(token_tile, "col", axis=0, tiled=True)
+    size = lax.axis_size("col")
+    pairs = [(i, (i + 1) % size) for i in range(size)]
+    back = [(b, a) for a, b in pairs]
+    lower, upper = ([], [])
+    for lap in range(size - 1):
+        if lap % 2 == 0:
+            lower.append(lax.ppermute(lower[-1] if lower else token_tile, "col", pairs))
+        else:
+            upper.append(lax.ppermute(upper[-1] if upper else token_tile, "col", back))
+    parts = jnp.stack([*lower[::-1], token_tile, *upper])
+    shift = lax.axis_index("col") - len(lower)
+    parts = parts[(jnp.arange(size) - shift) % size]
+    tokens_all = in_order(parts, 0)
     hidden_sum = lax.psum_scatter(
         jnp.dot(tokens_all, weight_tile, preferred_element_type=jnp.float32).astype(jnp.bfloat16),
         "row",

time: 81 us -> 81 us (level)
  blocking collectives: 19.7 us -> 13 us
  waiting for transfers between devices: 24.9 us -> 30.5 us
    ppermute x0 -> x3, waiting for transfers between devices: none -> 8.82 us  [the longest x2 8.82 us: on_device(): lower.append(lax.ppermute(lower[-1] if lower else token_tile, 'col', pairs))]
    all_gather x1 -> x0, blocking collectives: 6.64 us -> none  [on_device(): tokens_all = lax.all_gather(token_tile, 'col', axis=0, tiled=True)]
    reduce_scatter x1, waiting for transfers between devices: 11.9 us -> 8.71 us  [on_device(): lax.psum_scatter(input_piece, 'col', scatter_dimension=0, tiled=True)]
  transfers between devices with their start and end apart: 3 -> 6, of which waited for: 2 -> 4; matrix products, arithmetic and copies ran while one was open for 15% -> 16% of each run, Pallas kernels for 0% -> 0%
where the time goes in v1:
time: 81 us; the launch traced here: 80.7 us
  waiting for transfers between devices  30.5 us (38%)
  matrix products  18.9 us (23%)
  between operations  14.1 us (17%)
  blocking collectives  13 us (16%)
  starting transfers between devices  1.94 us (2%)
  local copies, waits for them, and re-layouts  1.22 us (2%)
  other arithmetic  1.01 us (1%)
    all_gather x1, blocking collectives, on_device(): grad_piece = lax.all_gather(grad_tile, 'row', axis=0, tiled=True)  13 us
    reduce_scatter x1, waiting for transfers between devices, on_device(): lax.psum_scatter(jnp.dot(tokens_all, weight_tile, preferred_element_type=...  12.9 us
    ppermute x2, waiting for transfers between devices, on_device(): lower.append(lax.ppermute(lower[-1] if lower else token_tile, 'col', pairs))  8.82 us
    reduce_scatter x1, waiting for transfers between devices, on_device(): lax.psum_scatter(input_piece, 'col', scatter_dimension=0, tiled=True)  8.71 us
    dot_general x1, matrix products, on_device(): lax.dot_general(grad_piece, weight_tile, (((1,), (1,)), ((), ())), prefer...  7.78 us
    dot_general x1, matrix products, on_device(): jnp.dot(tokens_all, weight_tile, preferred_element_type=jnp.float32)  5.98 us
    dot_general x1, matrix products, on_device(): lax.dot_general(tokens_all, grad_piece, (((0,), (0,)), ((), ())), preferr...  5.17 us
  transfers between devices with their start and end apart: 6, of which 4 were waited for; matrix products, arithmetic and copies ran while one was open for 16% of the time, Pallas kernels for 0%

profile of v1, /device:TPU:0, one launch (start us, length us, event | category | flops | bytes accessed | tf_op | source)
XLA Modules:
  0.0 80.7 jit_solution(4896896406643508303)
XLA Ops:
  7.2 0.0 copy-start
  7.2 0.0 reduce-scatter.5.cloned.1.call-start
  7.2 13.0 %all-gather = bf16[1,128,3072]{2,1,0:T(8,128)(2,1)S(1)} all-gather(bf16[1,64,3072]{2,1,0:T(8,128)(2,1)} %param.5), channel_id=2, replica_groups=mesh['section'=4,'row'=2,'col'=4] {'row'}, dimensions={1}, use_global_device_ids=true | all-gather | bytes 1179648 | tf_op jit(solution)/shard_map/all_gather | solution.py:42
  20.2 7.8 %fusion.1 = f32[128,1536]{1,0:T(8,128)} fusion(bf16[1,1536,3072]{2,1,0:T(8,128)(2,1)} %param.4, bf16[1,128,3072]{2,1,0:T(8,128)(2,1)S(1)} %all-gather), kind=kOutput, calls=%fused_computation.3 | convolution fusion | flops 1207959552 | bytes 11010048 | tf_op jit(solution)/shard_map/dot_general | solution.py:46
  28.0 0.0 reduce-scatter.5.cloned.1.call-update
  28.0 0.0 reduce-scatter.3.cloned.1.call-start
  28.1 0.0 copy-done
  28.1 0.3 collective-permute-start.2
  28.4 0.3 collective-permute-start
  28.7 4.8 %collective-permute-done = bf16[32,1536]{1,0:T(8,128)(2,1)S(1)} collective-permute-done((bf16[32,1536]{1,0:T(8,128)(2,1)S(1)}, bf16[32,1536]{1,0:T(8,128)(2,1)S(1)}, u32[]{:S(2)}, u32[]{:S(2)}) %collective-permute-start) | collective-permute-done | bytes 98336 | tf_op jit(solution)/shard_map/ppermute | solution.py:29
  33.5 0.0 collective-permute-start.1
  33.5 0.0 collective-permute-done.2
  33.5 4.0 %collective-permute-done.1 = bf16[32,1536]{1,0:T(8,128)(2,1)S(1)} collective-permute-done((bf16[32,1536]{1,0:T(8,128)(2,1)S(1)}, bf16[32,1536]{1,0:T(8,128)(2,1)S(1)}, u32[]{:S(2)}, u32[]{:S(2)}) %collective-permute-start.1) | collective-permute-done | bytes 98336 | tf_op jit(solution)/shard_map/ppermute | solution.py:29
  37.5 0.1 pad_maximum_fusion
  37.6 0.6 gather_fusion
  38.1 6.0 %fusion.5 = bf16[128,3072]{1,0:T(8,128)(2,1)} fusion(bf16[128,1536]{1,0:T(8,128)(2,1)S(1)} %bitcast.25, bf16[1,1536,3072]{2,1,0:T(8,128)(2,1)} %param.4), kind=kOutput, calls=%fused_computation.7 | convolution fusion | flops 1208352768 | bytes 10616832 | tf_op jit(solution)/shard_map/dot_general | solution.py:37
  44.1 0.0 reduce-scatter.3.cloned.1.call-update
  44.2 8.7 %reduce-scatter.5.cloned.1.call-done = f32[32,1536]{1,0:T(8,128)} async-done(((f32[128,1536]{1,0:T(8,128)}), f32[32,1536]{1,0:T(8,128)}) %reduce-scatter.5.cloned.1.call-update) | async-done | bytes 196624 | tf_op jit(solution)/shard_map/reduce_scatter | solution.py:50
  52.9 0.9 %convert_element_type.11 = bf16[32,1536]{1,0:T(8,128)(2,1)S(1)} convert(f32[32,1536]{1,0:T(8,128)} %reduce-scatter.5.cloned.1.call-done) | non-fusion elementwise | flops 49152 | bytes 294912 | tf_op jit(solution)/shard_map/convert_element_type | solution.py:50
  53.8 1.3 %collective-permute-start.3 = (bf16[32,1536]{1,0:T(8,128)(2,1)S(1)}, bf16[32,1536]{1,0:T(8,128)(2,1)S(1)}, u32[]{:S(2)}, u32[]{:S(2)}) collective-permute-start(bf16[32,1536]{1,0:T(8,128)(2,1)S(1)} %convert_element_type.11), channel_id=1, source_target_pairs={{8,0},{16,8},{24,16},{9,1},{17,9},{25,17},{10,2},{18,10},{26,18},{... | collective-permute-start | bytes 294920 | tf_op jit(solution)/shard_map/ppermute | solution.py:16
  55.1 5.2 %fusion = bf16[1,1536,3072]{2,1,0:T(8,128)(2,1)} fusion(bf16[128,1536]{1,0:T(8,128)(2,1)S(1)} %bitcast.26, bf16[1,128,3072]{2,1,0:T(8,128)(2,1)S(1)} %all-gather), kind=kOutput, calls=%fused_computation.2 | convolution fusion | flops 1212678144 | bytes 10616832 | tf_op jit(solution)/shard_map/dot_general | solution.py:43
  60.3 0.0 collective-permute-done.3
  60.3 12.9 %reduce-scatter.3.cloned.1.call-done = bf16[64,3072]{1,0:T(8,128)(2,1)} async-done(((bf16[128,3072]{1,0:T(8,128)(2,1)}), bf16[64,3072]{1,0:T(8,128)(2,1)}) %reduce-scatter.3.cloned.1.call-update) | async-done | bytes 393232 | tf_op jit(solution)/shard_map/reduce_scatter | solution.py:36
  73.3 0.6 copy.7
  (2 shorter events, 0.0 us)
Async XLA Ops:
  7.2 20.9 %copy-start = (bf16[1,32,1536]{2,1,0:T(8,128)(2,1)S(1)}, bf16[1,32,1536]{2,1,0:T(8,128)(2,1)}, u32[]{:S(2)}) copy-start(bf16[1,32,1536]{2,1,0:T(8,128)(2,1)} %param.3) | copy-start | bytes 294916
  7.2 45.7 %reduce-scatter.5.cloned.1.call-start = ((), (), s32[]{:S(2)}) async-start(), calls=%async_computation.3 | async-start | bytes 983040 | tf_op jit(solution)/shard_map/reduce_scatter | solution.py:50
  28.0 45.2 %reduce-scatter.3.cloned.1.call-start = ((), (), s32[]{:S(2)}) async-start(), calls=%async_computation.2 | async-start | bytes 1179648 | tf_op jit(solution)/shard_map/reduce_scatter | solution.py:36
  28.1 5.4 %collective-permute-start.2 = (bf16[32,1536]{1,0:T(8,128)(2,1)S(1)}, bf16[32,1536]{1,0:T(8,128)(2,1)S(1)}, u32[]{:S(2)}, u32[]{:S(2)}) collective-permute-start(bf16[32,1536]{1,0:T(8,128)(2,1)S(1)} %bitcast.27), channel_id=1, source_target_pairs={{1,0},{2,1},{3,2},{0,3},{5,4},{6,5},{7,6},{4,7},{9,8},{10,9},{11,1... | collective-permute-start | bytes 294920 | tf_op jit(solution)/shard_map/ppermute | solution.py:31
  28.4 5.1 %collective-permute-start = (bf16[32,1536]{1,0:T(8,128)(2,1)S(1)}, bf16[32,1536]{1,0:T(8,128)(2,1)S(1)}, u32[]{:S(2)}, u32[]{:S(2)}) collective-permute-start(bf16[32,1536]{1,0:T(8,128)(2,1)S(1)} %bitcast.28), channel_id=1, source_target_pairs={{0,1},{1,2},{2,3},{3,0},{4,5},{5,6},{6,7},{7,4},{8,9},{9,10},{10,1... | collective-permute-start | bytes 294920 | tf_op jit(solution)/shard_map/ppermute | solution.py:29
  33.5 4.0 %collective-permute-start.1 = (bf16[32,1536]{1,0:T(8,128)(2,1)S(1)}, bf16[32,1536]{1,0:T(8,128)(2,1)S(1)}, u32[]{:S(2)}, u32[]{:S(2)}) collective-permute-start(bf16[32,1536]{1,0:T(8,128)(2,1)S(1)} %collective-permute-done), channel_id=1, source_target_pairs={{0,1},{1,2},{2,3},{3,0},{4,5},{5,6},{6,7},{7,4},{8,9},{9,10},{10,1... | collective-permute-start | bytes 294920 | tf_op jit(solution)/shard_map/ppermute | solution.py:29
  53.8 6.5 %collective-permute-start.3 = (bf16[32,1536]{1,0:T(8,128)(2,1)S(1)}, bf16[32,1536]{1,0:T(8,128)(2,1)S(1)}, u32[]{:S(2)}, u32[]{:S(2)}) collective-permute-start(bf16[32,1536]{1,0:T(8,128)(2,1)S(1)} %convert_element_type.11), channel_id=1, source_target_pairs={{8,0},{16,8},{24,16},{9,1},{17,9},{25,17},{10,2},{18,10},{26,18},{... | collective-permute-start | bytes 294920 | tf_op jit(solution)/shard_map/ppermute | solution.py:16
Sparse Core Ops, SparseCore 0:
  28.2 24.6 reduce-scatter.4
  55.8 17.4 reduce-scatter.2
